TPU v7x, 32 devices: a whole 2x2x4 slice. The times are simulated.
32 devices in a mesh: iface: 8 (over z, core), sub: 4 (over y, x).
Axes of the slice: x: 2, y: 2, z: 4, core: 2. Of those that a mesh axis runs over, the one named last changes fastest.
Arguments:
- traces: bfloat16 [8, 32, 256, 256], P('iface', 'sub'), may hold values from -6 to 6
- elem_count: int32 [8, 32], P('iface', 'sub'), may hold values from 16 to 64, as said below
- near_idx: int32 [8, 32, 7], P('iface', 'sub'), may hold values from 0 to 31, as said below
- near_count: int32 [8, 32], P('iface', 'sub'), may hold values from 2 to 7, as said below
- near_blocks: bfloat16 [8, 32, 7, 256, 256], P('iface', 'sub'), may hold values from -0.125 to 0.125
- source_map: bfloat16 [8, 32, 128, 256], P('iface', 'sub'), may hold values from -0.125 to 0.125
- m2l_idx: int32 [8, 4, 3], P('iface', 'sub'), may hold values from 0 to 3, as said below
- m2l_count: int32 [8, 4], P('iface', 'sub'), may hold values from 2 to 3, as said below
- translate: bfloat16 [8, 4, 3, 128, 128], P('iface', 'sub'), may hold values from -0.3125 to 0.3125
- evaluate: bfloat16 [8, 32, 256, 128], P('iface', 'sub'), may hold values from -0.5 to 0.5
- send_idx: int32 [8, 4, 2, 4, 16], P('iface', 'sub'), may hold values from 0 to 511
- recv_idx: int32 [8, 4, 2, 4, 16], P('iface', 'sub'), may hold values from 0 to 511
- recv_count: int32 [8, 4, 2, 4], P('iface', 'sub'), may hold values from 0 to 16, as said below
- couple_weight: float32 [8, 4, 2, 4, 16], P('iface', 'sub'), may hold values from 0.25 to 2
Outputs:
- calderon: bfloat16 [8, 32, 256, 256], P('iface', 'sub')
Inputs may be any that keep to these rules, and one draw needn't show every extreme that they name: `near_idx`: each slot names a leaf of the same cluster at most 3 leaves from its own; slot 0 is the leaf 3 before and slot 1 the leaf 3 after, clipped to the cluster. `near_count`: some leaf of every cluster has all slots live. `elem_count`: some leaf of every cluster is full. `m2l_idx`: the slots of a box name every other box of its cluster once each. `m2l_count`: some box of every cluster has all slots live. `recv_count`: for every receiving box and side, one sending box fills all 16 slots.
All inputs are finite; a program needn't handle non-finite values.
Results may differ from a plain program's by a relative error of at most 0.0044.
Values may be sent and summed in bfloat16 or wider, within the bound.
No kernel may reach another device: no remote copies, remote signals or barrier semaphores. Data moves between devices by JAX's collectives and lax.ppermute only.
A program may use at most 64 MiB of HBM per device.

v0:
```python
import jax
import jax.numpy as jnp
from jax import lax
from jax.sharding import PartitionSpec as P

REACH = 3


def with_halo(block, sides, width):
    for axis, dim in sides:
        count = lax.axis_size(axis)
        forward = [(i, i + 1) for i in range(count - 1)]
        backward = [(target, source) for source, target in forward]
        low = lax.ppermute(
            lax.slice_in_dim(block, block.shape[dim] - width, None, axis=dim), axis, forward
        )
        high = lax.ppermute(lax.slice_in_dim(block, 0, width, axis=dim), axis, backward)
        block = jnp.concatenate([low, block, high], axis=dim)
    return block


def shifted(shard, axis, by):
    count = lax.axis_size(axis)
    pairs = [(i, i + by) for i in range(count) if 0 <= i + by < count]
    return lax.ppermute(shard, axis, pairs)


def shards(
    traces,
    elem_count,
    near_idx,
    near_count,
    near_blocks,
    source_map,
    m2l_idx,
    m2l_count,
    translate,
    evaluate,
    send_idx,
    recv_idx,
    recv_count,
    couple_weight,
):
    leaves_here = traces.shape[1]
    row_count = traces.shape[2]
    leaf_size = row_count // 4
    fields = traces.shape[3]
    positions = jnp.arange(leaf_size, dtype=jnp.int32)
    live_leaf = positions[None, :] < elem_count[0][:, None]
    live_rows = jnp.tile(live_leaf, (1, 4))
    masked = jnp.where(live_rows[:, :, None], traces[0], jnp.zeros((), traces.dtype))
    padded = with_halo(masked, (("sub", 0),), REACH)
    my_index = lax.axis_index("sub")
    local_idx = near_idx[0] - my_index * leaves_here + REACH
    picked = padded[local_idx]
    slot_count = near_idx.shape[2]
    slot_live = jnp.arange(slot_count, dtype=jnp.int32)[None, :] < near_count[0][:, None]
    picked = jnp.where(slot_live[:, :, None, None], picked, jnp.zeros((), picked.dtype))
    near_part = jnp.einsum(
        "lsij,lsjn->lin", near_blocks[0], picked, preferred_element_type=jnp.float32
    )
    moment = jnp.einsum(
        "lqj,ljn->qn", source_map[0], masked, preferred_element_type=jnp.float32
    ).astype(jnp.bfloat16)
    wanted = m2l_idx[0, 0]
    trans_slots = wanted.shape[0]
    all_boxes = lax.all_gather(moment[None], "sub", axis=0, tiled=True)
    chosen = all_boxes[wanted]
    m2l_live = jnp.arange(trans_slots, dtype=jnp.int32) < m2l_count[0, 0]
    chosen = jnp.where(m2l_live[:, None, None], chosen, jnp.zeros((), chosen.dtype))
    box_local = jnp.einsum(
        "mpq,mqn->pn", translate[0, 0], chosen, preferred_element_type=jnp.float32
    ).astype(jnp.bfloat16)
    far_part = jnp.einsum("liq,qn->lin", evaluate[0], box_local, preferred_element_type=jnp.float32)
    element_count = leaves_here * leaf_size
    elements = (
        masked.reshape(leaves_here, 4, leaf_size, fields)
        .transpose(0, 2, 1, 3)
        .reshape(element_count, 4, fields)
    )
    outgoing = elements[send_idx[0, 0]]
    owned = lax.all_to_all(outgoing, "sub", split_axis=1, concat_axis=1, tiled=True)
    from_left = shifted(owned[1], "iface", 1)
    from_right = shifted(owned[0], "iface", -1)
    arrived = jnp.stack([from_left, from_right], axis=0)
    slot_total = recv_idx.shape[4]
    slot_valid = (
        jnp.arange(slot_total, dtype=jnp.int32)[None, None, :] < recv_count[0, 0][:, :, None]
    )
    weights = jnp.where(slot_valid, couple_weight[0, 0], jnp.zeros((), jnp.float32))
    sign_row = jnp.array([1.0, 1.0, -1.0, -1.0], dtype=jnp.float32)
    scaled = arrived.astype(jnp.float32) * weights[..., None, None] * sign_row[:, None]
    targets = recv_idx[0, 0].reshape(-1)
    iface_el = (
        jnp.zeros((element_count, 4, fields), jnp.float32)
        .at[targets]
        .add(scaled.reshape(-1, 4, fields))
    )
    iface_part = (
        iface_el.reshape(leaves_here, leaf_size, 4, fields)
        .transpose(0, 2, 1, 3)
        .reshape(leaves_here, row_count, fields)
    )
    total = near_part + far_part + iface_part
    result = jnp.where(live_rows[:, :, None], total, jnp.zeros((), jnp.float32)).astype(
        jnp.bfloat16
    )
    return result[None]


def solution(mesh):
    return jax.shard_map(
        shards,
        mesh=mesh,
        in_specs=(
            P("iface", "sub", None, None),
            P("iface", "sub"),
            P("iface", "sub", None),
            P("iface", "sub"),
            P("iface", "sub", None, None, None),
            P("iface", "sub", None, None),
            P("iface", "sub", None),
            P("iface", "sub"),
            P("iface", "sub", None, None, None),
            P("iface", "sub", None, None),
            P("iface", "sub", None, None, None),
            P("iface", "sub", None, None, None),
            P("iface", "sub", None, None),
            P("iface", "sub", None, None, None),
        ),
        out_specs=P("iface", "sub", None, None),
        check_vma=False,
    )
```

profile of v0, /device:TPU:1, one launch (start us, length us, event | category | flops | bytes accessed | tf_op | source)
XLA Modules:
  0.0 85.5 jit_solution(13542415011376778090)
XLA Ops:
  0.0 0.8 iota_compare_fusion.2
  0.8 0.1 tile.9
  0.9 1.5 %copy.37 = bf16[1,8,256,256]{2,3,1,0:T(8,128)(2,1)S(1)} copy(bf16[1,8,256,256]{3,2,1,0:T(8,128)(2,1)} %param.15) | data formatting | bytes 2097152 | tf_op args[0]
  2.5 0.9 %fusion.38 = (bf16[3,256,256]{1,2,0:T(8,128)(2,1)}, bf16[3,256,256]{1,2,0:T(8,128)(2,1)}) fusion(bf16[8,256,256]{1,2,0:T(8,128)(2,1)S(1)} %bitcast_select_fusion), kind=kLoop, calls=%fused_computation.51 | loop fusion | bytes 1572864 | tf_op jit(solution)/shard_map/slice | solution.py:15
  3.4 4.7 %collective-permute-start = (bf16[3,256,256]{1,2,0:T(8,128)(2,1)}, bf16[3,256,256]{1,2,0:T(8,128)(2,1)}, u32[]{:S(2)}, u32[]{:S(2)}) collective-permute-start(bf16[3,256,256]{1,2,0:T(8,128)(2,1)} %get-tuple-element.5), channel_id=1, source_target_pairs={{0,1},{1,2},{2,3},{4,5},{5,6},{6,7},{8,9},{9,10},{10,11},{12,13},{... | collective-permute-start | bytes 1179656 | tf_op jit(solution)/shard_map/ppermute | solution.py:14
  8.1 1.3 %collective-permute-start.1 = (bf16[3,256,256]{1,2,0:T(8,128)(2,1)}, bf16[3,256,256]{1,2,0:T(8,128)(2,1)}, u32[]{:S(2)}, u32[]{:S(2)}) collective-permute-start(bf16[3,256,256]{1,2,0:T(8,128)(2,1)} %get-tuple-element.6), channel_id=1, source_target_pairs={{1,0},{2,1},{3,2},{5,4},{6,5},{7,6},{9,8},{10,9},{11,10},{13,12},{... | collective-permute-start | bytes 1179656 | tf_op jit(solution)/shard_map/ppermute | solution.py:17
  9.4 0.1 select_bitcast_fusion
  9.5 0.1 copy.41
  9.7 0.8 copy.42
  10.7 0.8 gather_fusion.2
  11.5 0.8 copy.43
  12.3 4.3 %all-to-all-start = ((bf16[2,4,16,4,256]{4,3,2,0,1:T(4,128)(2,1)}), bf16[2,4,16,4,256]{4,3,2,0,1:T(4,128)(2,1)S(1)}, u32[]{:S(2)}, u32[]{:S(2)}) async-start(bf16[2,4,16,4,256]{4,3,2,0,1:T(4,128)(2,1)} %copy.43), calls=%async_computation | async-start | bytes 524288 | tf_op jit(solution)/shard_map/all_to_all | solution.py:82
  17.0 0.4 fusion.19
  17.4 15.0 %all-gather = bf16[512,256]{0,1:T(8,128)(2,1)S(1)} all-gather(bf16[128,256]{0,1:T(8,128)(2,1)S(1)} %fusion.19), channel_id=2, replica_groups=mesh['iface'=8,'sub'=4] {'sub'}, dimensions={0}, use_global_device_ids=true | all-gather | bytes 327680 | tf_op jit(solution)/shard_map/all_gather | solution.py:67
  32.5 0.1 copy.51
  33.4 0.6 gather_fusion.1
  34.0 2.1 %fusion.21 = f32[256,8,256]{2,0,1:T(8,128)} fusion(bf16[1,8,256,128]{3,2,1,0:T(8,128)(2,1)S(1)} %copy-done, bf16[3,128,256]{2,1,0:T(8,128)(2,1)S(1)} %gather_fusion.1, pred[3]{0:T(512)(128)(4,1)S(1)} %iota_compare_fusion.3, bf16[1,1,3,128,128]{4,3,2,1,0:T(8,128)(2,1)S(1)} %copy-done.3), kind=kOutput, calls=%fused_computation.23 | convolution fusion | flops 159514624 | bytes 2916355 | tf_op jit(solution)/shard_map/liq,qn->lin/dot_general | solution.py:74
  36.1 0.1 slice_bitcast_fusion.1
  36.2 4.6 %collective-permute-start.2 = (bf16[4,16,4,256]{3,2,1,0:T(4,128)(2,1)S(1)}, bf16[4,16,4,256]{3,2,1,0:T(4,128)(2,1)S(1)}, u32[]{:S(2)}, u32[]{:S(2)}) collective-permute-start(bf16[4,16,4,256]{3,2,1,0:T(4,128)(2,1)S(1)} %get-tuple-element.7), channel_id=1, source_target_pairs={{0,4},{4,8},{8,12},{12,16},{16,20},{20,24},{24,28},{1,5},{5,9},{9,... | collective-permute-start | bytes 393224 | tf_op jit(solution)/shard_map/ppermute | solution.py:25
  40.8 1.9 %collective-permute-start.3 = (bf16[4,16,4,256]{3,2,1,0:T(4,128)(2,1)S(1)}, bf16[4,16,4,256]{3,2,1,0:T(4,128)(2,1)S(1)}, u32[]{:S(2)}, u32[]{:S(2)}) collective-permute-start(bf16[4,16,4,256]{3,2,1,0:T(4,128)(2,1)S(1)} %get-tuple-element.8), channel_id=1, source_target_pairs={{4,0},{8,4},{12,8},{16,12},{20,16},{24,20},{28,24},{5,1},{9,5},{13... | collective-permute-start | bytes 393224 | tf_op jit(solution)/shard_map/ppermute | solution.py:25
  42.9 4.2 %collective-permute-done.3 = bf16[4,16,4,256]{3,2,1,0:T(4,128)(2,1)S(1)} collective-permute-done((bf16[4,16,4,256]{3,2,1,0:T(4,128)(2,1)S(1)}, bf16[4,16,4,256]{3,2,1,0:T(4,128)(2,1)S(1)}, u32[]{:S(2)}, u32[]{:S(2)}) %collective-permute-start.3) | collective-permute-done | bytes 131104 | tf_op jit(solution)/shard_map/ppermute | solution.py:25
  47.1 0.2 pad_maximum_fusion.1
  47.3 0.2 fusion.22
  47.5 1.6 %broadcast_in_dim.80 = f32[512,4,256]{2,1,0:T(4,128)} broadcast(f32[]{:T(128)} %constant.4.clone.1), dimensions={} | broadcast | bytes 2097156 | tf_op jit(solution)/shard_map/broadcast_in_dim | solution.py:95
  49.1 13.6 %scatter_fusion = f32[512,4,256]{2,1,0:T(4,128)} fusion(f32[512,4,256]{2,1,0:T(4,128)} %broadcast_in_dim.80, s32[128]{0:T(128)S(1)} %fusion.34, f32[128,4,256]{2,1,0:T(4,128)S(1)} %fusion.22), kind=kCustom, calls=%fused_computation.3 | custom fusion | flops 131072 | bytes 1573376 | tf_op jit(solution)/shard_map/scatter-add | solution.py:97
  62.7 2.0 %copy.45 = f32[512,4,256]{2,0,1:T(8,128)S(1)} copy(f32[512,4,256]{2,1,0:T(4,128)} %scatter_fusion) | data formatting | bytes 4194304 | tf_op jit(solution)/shard_map/scatter-add | solution.py:97
  64.7 1.5 %copy.46 = f32[8,4,64,256]{3,2,1,0:T(8,128)} copy(f32[8,4,64,256]{3,2,0,1:T(8,128)S(1)} %bitcast.102) | data formatting | bytes 4194304 | tf_op jit(solution)/shard_map/transpose | solution.py:101
  66.2 2.9 %copy.47 = f32[8,256,256]{1,2,0:T(8,128)} copy(f32[8,256,256]{2,1,0:T(8,128)} %bitcast.103) | data formatting | bytes 4194304 | tf_op jit(solution)/shard_map/reshape | solution.py:102
  69.1 1.3 %pad_maximum_fusion = bf16[14,256,256]{1,2,0:T(8,128)(2,1)S(1)} fusion(bf16[3,256,256]{1,2,0:T(8,128)(2,1)} %collective-permute-done.1, bf16[8,256,256]{1,2,0:T(8,128)(2,1)S(1)} %bitcast_select_fusion, bf16[3,256,256]{1,2,0:T(8,128)(2,1)} %collective-permute-done), kind=kLoop, calls=%fused_computation.13 | loop fusion | flops 1835008 | bytes 3670016 | tf_op jit(solution)/shard_map/concatenate | solution.py:18
  70.4 5.2 %gather_fusion = bf16[56,256,256]{1,2,0:T(8,128)(2,1)} fusion(bf16[14,256,256]{1,2,0:T(8,128)(2,1)S(1)} %pad_maximum_fusion, s32[1024]{0:T(1024)S(1)} %pad_clamp_fusion.2), kind=kCustom, calls=%fused_computation | custom fusion | bytes 14680288 | tf_op jit(solution)/shard_map/gather | solution.py:55
  75.6 8.6 %fusion.12 = bf16[1,8,256,256]{2,3,1,0:T(8,128)(2,1)S(1)} fusion(f32[8,256,256]{1,2,0:T(8,128)} %copy.47, f32[256,8,256]{2,0,1:T(8,128)} %fusion.21, bf16[1,8,7,256,256]{4,3,2,1,0:T(8,128)(2,1)} %param.19, bf16[8,7,256,256]{2,3,1,0:T(8,128)(2,1)} %bitcast.104, pred[8,7]{1,0:T(8,128)(4,1)S(1)} %iota_compare_fusion.1, pred[8,256]{1,0:T(8,128)(4,1)S(1)} %tile.9), kind=kOutput, calls=%fused_computation.14 | convolution fusion | flops 1884815360 | bytes 19925048 | tf_op jit(solution)/shard_map/lsij,lsjn->lin/dot_general | solution.py:59
  84.2 1.3 %copy.48 = bf16[1,8,256,256]{3,2,1,0:T(8,128)(2,1)} copy(bf16[1,8,256,256]{2,3,1,0:T(8,128)(2,1)S(1)} %fusion.12) | data formatting | bytes 2097152 | tf_op jit(solution)/shard_map/broadcast_in_dim | solution.py:108
  (47 shorter events, 0.9 us)
Async XLA Ops:
  0.0 34.0 %copy-start = (bf16[1,8,256,128]{3,2,1,0:T(8,128)(2,1)S(1)}, bf16[1,8,256,128]{3,2,1,0:T(8,128)(2,1)}, u32[]{:S(2)}) copy-start(bf16[1,8,256,128]{3,2,1,0:T(8,128)(2,1)} %param.24) | copy-start | bytes 1572868
  2.4 7.0 %copy-start.1 = (bf16[1,8,256,256]{3,2,1,0:T(8,128)(2,1)S(1)}, bf16[1,8,256,256]{3,2,1,0:T(8,128)(2,1)}, u32[]{:S(2)}) copy-start(bf16[1,8,256,256]{3,2,1,0:T(8,128)(2,1)} %param.15) | copy-start | bytes 3145732
  3.4 65.7 %collective-permute-start = (bf16[3,256,256]{1,2,0:T(8,128)(2,1)}, bf16[3,256,256]{1,2,0:T(8,128)(2,1)}, u32[]{:S(2)}, u32[]{:S(2)}) collective-permute-start(bf16[3,256,256]{1,2,0:T(8,128)(2,1)} %get-tuple-element.5), channel_id=1, source_target_pairs={{0,1},{1,2},{2,3},{4,5},{5,6},{6,7},{8,9},{9,10},{10,11},{12,13},{... | collective-permute-start | bytes 1179656 | tf_op jit(solution)/shard_map/ppermute | solution.py:14
  8.1 61.0 %collective-permute-start.1 = (bf16[3,256,256]{1,2,0:T(8,128)(2,1)}, bf16[3,256,256]{1,2,0:T(8,128)(2,1)}, u32[]{:S(2)}, u32[]{:S(2)}) collective-permute-start(bf16[3,256,256]{1,2,0:T(8,128)(2,1)} %get-tuple-element.6), channel_id=1, source_target_pairs={{1,0},{2,1},{3,2},{5,4},{6,5},{7,6},{9,8},{10,9},{11,10},{13,12},{... | collective-permute-start | bytes 1179656 | tf_op jit(solution)/shard_map/ppermute | solution.py:17
  9.5 1.0 %copy-start.6 = (s32[1,1,2,4,16]{4,3,2,1,0:T(4,128)S(1)}, s32[1,1,2,4,16]{4,3,2,1,0:T(4,128)}, u32[]{:S(2)}) copy-start(s32[1,1,2,4,16]{4,3,2,1,0:T(4,128)} %param.25) | copy-start | bytes 1540
  9.7 7.0 %copy-start.8 = (s32[1,1,2,4]{3,2,1,0:T(2,128)S(1)}, s32[1,1,2,4]{3,2,1,0:T(2,128)}, u32[]{:S(2)}) copy-start(s32[1,1,2,4]{3,2,1,0:T(2,128)} %param.27) | copy-start | bytes 100
  9.7 7.1 %copy-start.4 = (f32[1,1,2,4,16]{4,3,2,1,0:T(4,128)S(1)}, f32[1,1,2,4,16]{4,3,2,1,0:T(4,128)}, u32[]{:S(2)}) copy-start(f32[1,1,2,4,16]{4,3,2,1,0:T(4,128)} %param.28) | copy-start | bytes 1540
  9.7 7.2 %copy-start.5 = (s32[1,1,2,4,16]{4,3,2,1,0:T(4,128)S(1)}, s32[1,1,2,4,16]{4,3,2,1,0:T(4,128)}, u32[]{:S(2)}) copy-start(s32[1,1,2,4,16]{4,3,2,1,0:T(4,128)} %param.26) | copy-start | bytes 1540
  9.7 7.3 %copy-start.2 = (bf16[1,8,128,256]{3,2,1,0:T(8,128)(2,1)S(1)}, bf16[1,8,128,256]{3,2,1,0:T(8,128)(2,1)}, u32[]{:S(2)}) copy-start(bf16[1,8,128,256]{3,2,1,0:T(8,128)(2,1)} %param.20) | copy-start | bytes 1572868
  10.5 22.1 %copy-start.10 = (s32[1,1,3]{2,1,0:T(1,128)S(1)}, s32[1,1,3]{2,1,0:T(1,128)}, u32[]{:S(2)}) copy-start(s32[1,1,3]{2,1,0:T(1,128)} %param.21) | copy-start | bytes 40
  10.5 22.8 %copy-start.11 = (s32[1,8]{1,0:T(1,128)S(1)}, s32[1,8]{1,0:T(1,128)}, u32[]{:S(2)}) copy-start(s32[1,8]{1,0:T(1,128)} %param.18) | copy-start | bytes 100
  10.6 22.8 %copy-start.7 = (s32[1,8,7]{1,0,2:T(1,128)S(1)}, s32[1,8,7]{1,0,2:T(1,128)}, u32[]{:S(2)}) copy-start(s32[1,8,7]{1,0,2:T(1,128)} %param.17) | copy-start | bytes 676
  11.5 22.5 %copy-start.3 = (bf16[1,1,3,128,128]{4,3,2,1,0:T(8,128)(2,1)S(1)}, bf16[1,1,3,128,128]{4,3,2,1,0:T(8,128)(2,1)}, u32[]{:S(2)}) copy-start(bf16[1,1,3,128,128]{4,3,2,1,0:T(8,128)(2,1)} %param.23) | copy-start | bytes 294916
  12.3 23.8 %all-to-all-start = ((bf16[2,4,16,4,256]{4,3,2,0,1:T(4,128)(2,1)}), bf16[2,4,16,4,256]{4,3,2,0,1:T(4,128)(2,1)S(1)}, u32[]{:S(2)}, u32[]{:S(2)}) async-start(bf16[2,4,16,4,256]{4,3,2,0,1:T(4,128)(2,1)} %copy.43), calls=%async_computation | async-start | bytes 524288 | tf_op jit(solution)/shard_map/all_to_all | solution.py:82
  33.4 13.9 %copy-start.9 = (f32[4]{0:T(128)S(1)}, f32[4]{0:T(128)}, u32[]{:S(2)}) copy-start(f32[4]{0:T(128)} %constant.6.clone) | copy-start | bytes 52
  36.2 6.7 %collective-permute-start.2 = (bf16[4,16,4,256]{3,2,1,0:T(4,128)(2,1)S(1)}, bf16[4,16,4,256]{3,2,1,0:T(4,128)(2,1)S(1)}, u32[]{:S(2)}, u32[]{:S(2)}) collective-permute-start(bf16[4,16,4,256]{3,2,1,0:T(4,128)(2,1)S(1)} %get-tuple-element.7), channel_id=1, source_target_pairs={{0,4},{4,8},{8,12},{12,16},{16,20},{20,24},{24,28},{1,5},{5,9},{9,... | collective-permute-start | bytes 393224 | tf_op jit(solution)/shard_map/ppermute | solution.py:25
  40.8 6.3 %collective-permute-start.3 = (bf16[4,16,4,256]{3,2,1,0:T(4,128)(2,1)S(1)}, bf16[4,16,4,256]{3,2,1,0:T(4,128)(2,1)S(1)}, u32[]{:S(2)}, u32[]{:S(2)}) collective-permute-start(bf16[4,16,4,256]{3,2,1,0:T(4,128)(2,1)S(1)} %get-tuple-element.8), channel_id=1, source_target_pairs={{4,0},{8,4},{12,8},{16,12},{20,16},{24,20},{28,24},{5,1},{9,5},{13... | collective-permute-start | bytes 393224 | tf_op jit(solution)/shard_map/ppermute | solution.py:25
where the time goes:
time: 86.2 us; the launch traced here: 85.5 us
  local copies, waits for them, and re-layouts  20.9 us (24%)
  starting transfers between devices  16.8 us (19%)
  other arithmetic  16.5 us (19%)
  blocking collectives  15 us (17%)
  matrix products  11.1 us (13%)
  waiting for transfers between devices  4.18 us (5%)
  between operations  0.98 us (1%)
    all_gather x1, blocking collectives, shards(): all_boxes = lax.all_gather(moment[None], 'sub', axis=0, tiled=True)  15 us
    scatter-add x1, other arithmetic, shards(): iface_el = jnp.zeros((element_count, 4, fields), jnp.float32).at[targets]...  13.6 us
    dot_general x1, matrix products, shards(): jnp.einsum('lsij,lsjn->lin', near_blocks[0], picked, preferred_element_ty...  8.57 us
    ppermute x2, starting transfers between devices, shifted(): return lax.ppermute(shard, axis, pairs)  6.51 us
    gather x1, local copies, waits for them, and re-layouts, shards(): picked = padded[local_idx]  5.24 us
    ppermute x1, starting transfers between devices, with_halo(): lax.ppermute(lax.slice_in_dim(block, block.shape[dim] - width, None, axis...  4.69 us
    all_to_all x1, starting transfers between devices, shards(): lax.all_to_all(outgoing, 'sub', split_axis=1, concat_axis=1, tiled=True)  4.32 us
    ppermute x2, waiting for transfers between devices, shifted(): return lax.ppermute(shard, axis, pairs)  4.17 us
  transfers between devices with their start and end apart: 5, of which 1 were waited for; matrix products, arithmetic and copies ran while one was open for 34% of the time, Pallas kernels for 0%

commit v1 on v0

--- a/solution.py
+++ b/solution.py
@@ -79,7 +79,19 @@
         .reshape(element_count, 4, fields)
     )
     outgoing = elements[send_idx[0, 0]]
-    owned = lax.all_to_all(outgoing, "sub", split_axis=1, concat_axis=1, tiled=True)
+    ways, here = (lax.axis_size("sub"), lax.axis_index("sub"))
+    width_2 = outgoing.shape[1] // ways
+    dims = list(outgoing.shape)
+    dims[1] = width_2
+    height = dims[1]
+    dims[1] = height * ways
+    full = jnp.zeros(dims, outgoing.dtype)
+    for mask in range(ways):
+        part = lax.dynamic_slice_in_dim(outgoing, (here ^ mask) * width_2, width_2, axis=1)
+        if mask:
+            part = lax.ppermute(part, "sub", [(d, d ^ mask) for d in range(ways)])
+        full = lax.dynamic_update_slice_in_dim(full, part, (here ^ mask) * height, axis=1)
+    owned = full
     from_left = shifted(owned[1], "iface", 1)
     from_right = shifted(owned[0], "iface", -1)
     arrived = jnp.stack([from_left, from_right], axis=0)

time: 86.2 us -> 95.9 us (1.11)
  other arithmetic: 16.5 us -> 21.3 us
  local copies, waits for them, and re-layouts: 20.9 us -> 23.6 us
  matrix products: 11.1 us -> 13 us
    all_to_all x1 -> x0, starting transfers between devices: 4.32 us -> none  [shards(): lax.all_to_all(outgoing, 'sub', split_axis=1, concat_axis=1, tiled=True)]
    ppermute x0 -> x3, starting transfers between devices: none -> 3.28 us  [shards(): part = lax.ppermute(part, 'sub', [(d, d ^ mask) for d in range(ways)])]
    dynamic_update_slice x0 -> x3, local copies, waits for them, and re-layouts: none -> 2.64 us  [shards(): lax.dynamic_update_slice_in_dim(full, part, (here ^ mask) * height, axis=1)]
    ppermute x2, starting transfers between devices: 6.51 us -> 8.54 us  [shifted(): return lax.ppermute(shard, axis, pairs)]
    ppermute x1, starting transfers between devices: 4.69 us -> 3.33 us  [with_halo(): lax.ppermute(lax.slice_in_dim(block, block.shape[dim] - width, None, axis...]
    transpose x1, other arithmetic: 0.14 us -> 1.37 us  [shards(): elements = masked.reshape(leaves_here, 4, leaf_size, fields).transpose(0,...]
    lt x1, other arithmetic: 0.07 us -> 1.27 us  [shards(): jnp.arange(slot_count, dtype=jnp.int32)[None, :] < near_count[0][:, None]]
    select_n x1, other arithmetic: 0.01 us -> 1.17 us  [shards(): jnp.where(slot_valid, couple_weight[0, 0], jnp.zeros((), jnp.float32))]
  transfers between devices with their start and end apart: 5 -> 7, of which waited for: 1 -> 1; matrix products, arithmetic and copies ran while one was open for 34% -> 38% of each run, Pallas kernels for 0% -> 0%
where the time goes in v1:
time: 95.9 us; the launch traced here: 94.8 us
  local copies, waits for them, and re-layouts  23.6 us (25%)
  other arithmetic  21.3 us (22%)
  starting transfers between devices  16.4 us (17%)
  blocking collectives  15.3 us (16%)
  matrix products  13 us (14%)
  waiting for transfers between devices  4.18 us (4%)
  between operations  0.98 us (1%)
    all_gather x1, blocking collectives, shards(): all_boxes = lax.all_gather(moment[None], 'sub', axis=0, tiled=True)  15.3 us
    scatter-add x1, other arithmetic, shards(): iface_el = jnp.zeros((element_count, 4, fields), jnp.float32).at[targets]...  13.6 us
    dot_general x1, matrix products, shards(): jnp.einsum('lsij,lsjn->lin', near_blocks[0], picked, preferred_element_ty...  8.56 us
    ppermute x2, starting transfers between devices, shifted(): return lax.ppermute(shard, axis, pairs)  8.54 us
    gather x1, local copies, waits for them, and re-layouts, shards(): picked = padded[local_idx]  5.24 us
    ppermute x2, waiting for transfers between devices, shifted(): return lax.ppermute(shard, axis, pairs)  4.17 us
    ppermute x1, starting transfers between devices, with_halo(): lax.ppermute(lax.slice_in_dim(block, block.shape[dim] - width, None, axis...  3.33 us
    ppermute x3, starting transfers between devices, shards(): part = lax.ppermute(part, 'sub', [(d, d ^ mask) for d in range(ways)])  3.28 us
  transfers between devices with their start and end apart: 7, of which 1 were waited for; matrix products, arithmetic and copies ran while one was open for 38% of the time, Pallas kernels for 0%

profile of v1, /device:TPU:1, one launch (start us, length us, event | category | flops | bytes accessed | tf_op | source)
XLA Modules:
  0.0 94.8 jit_solution(1708413624530915024)
XLA Ops:
  0.0 0.8 iota_compare_fusion.2
  0.8 1.4 %select_bitcast_fusion = bf16[8,64,4,256]{3,1,2,0:T(8,128)(2,1)S(1)} fusion(bf16[8,4,64,256]{3,2,1,0:T(8,128)(2,1)} %bitcast.104, pred[8,64]{1,0:T(8,128)(4,1)S(1)} %iota_compare_fusion.2), kind=kLoop, calls=%fused_computation.22 | loop fusion | flops 524288 | bytes 2097664 | tf_op jit(solution)/shard_map/transpose | solution.py:78
  2.3 0.8 copy.35
  3.2 0.8 gather_fusion.2
  4.1 0.8 constant_dynamic-slice_fusion
  4.9 2.0 %collective-permute-start.2 = (bf16[2,1,16,4,256]{4,3,2,1,0:T(4,128)(2,1)}, bf16[2,1,16,4,256]{4,3,2,1,0:T(4,128)(2,1)}, u32[]{:S(2)}, u32[]{:S(2)}) collective-permute-start(bf16[2,1,16,4,256]{4,3,2,1,0:T(4,128)(2,1)} %get-tuple-element.11), channel_id=1, source_target_pairs={{0,1},{1,0},{2,3},{3,2},{4,5},{5,4},{6,7},{7,6},{8,9},{9,8},{10,11... | collective-permute-start | bytes 196616 | tf_op jit(solution)/shard_map/ppermute | solution.py:92
  6.9 1.2 %collective-permute-start.3 = (bf16[2,1,16,4,256]{4,3,2,1,0:T(4,128)(2,1)}, bf16[2,1,16,4,256]{4,3,2,1,0:T(4,128)(2,1)}, u32[]{:S(2)}, u32[]{:S(2)}) collective-permute-start(bf16[2,1,16,4,256]{4,3,2,1,0:T(4,128)(2,1)} %get-tuple-element.10), channel_id=1, source_target_pairs={{0,2},{1,3},{2,0},{3,1},{4,6},{5,7},{6,4},{7,5},{8,10},{9,11},{10,... | collective-permute-start | bytes 196616 | tf_op jit(solution)/shard_map/ppermute | solution.py:92
  9.0 3.3 %collective-permute-start = (bf16[3,256,256]{1,2,0:T(8,128)(2,1)S(1)}, bf16[3,256,256]{1,2,0:T(8,128)(2,1)S(1)}, u32[]{:S(2)}, u32[]{:S(2)}) collective-permute-start(bf16[3,256,256]{1,2,0:T(8,128)(2,1)S(1)} %get-tuple-element.5), channel_id=1, source_target_pairs={{0,1},{1,2},{2,3},{4,5},{5,6},{6,7},{8,9},{9,10},{10,11},{12,13},{... | collective-permute-start | bytes 1179656 | tf_op jit(solution)/shard_map/ppermute | solution.py:14
  12.3 1.3 %collective-permute-start.1 = (bf16[3,256,256]{1,2,0:T(8,128)(2,1)S(1)}, bf16[3,256,256]{1,2,0:T(8,128)(2,1)}, u32[]{:S(2)}, u32[]{:S(2)}) collective-permute-start(bf16[3,256,256]{1,2,0:T(8,128)(2,1)S(1)} %get-tuple-element.6), channel_id=1, source_target_pairs={{1,0},{2,1},{3,2},{5,4},{6,5},{7,6},{9,8},{10,9},{11,10},{13,12},{... | collective-permute-start | bytes 1179656 | tf_op jit(solution)/shard_map/ppermute | solution.py:17
  13.7 0.7 lt.160
  15.0 1.5 %fusion.19 = bf16[128,256]{0,1:T(8,128)(2,1)S(1)} fusion(bf16[8,256,256]{1,2,0:T(8,128)(2,1)S(1)} %bitcast_select_fusion, bf16[1,8,128,256]{3,2,1,0:T(8,128)(2,1)} %param.20), kind=kOutput, calls=%fused_computation.19 | convolution fusion | flops 134250496 | bytes 1638400 | tf_op jit(solution)/shard_map/lqj,ljn->qn/dot_general | solution.py:62
  16.5 15.3 %all-gather = bf16[512,256]{0,1:T(8,128)(2,1)S(1)} all-gather(bf16[128,256]{0,1:T(8,128)(2,1)S(1)} %fusion.19), channel_id=2, replica_groups=mesh['iface'=8,'sub'=4] {'sub'}, dimensions={0}, use_global_device_ids=true | all-gather | bytes 327680 | tf_op jit(solution)/shard_map/all_gather | solution.py:67
  33.2 1.3 %iota_compare_fusion.1 = pred[8,7]{1,0:T(8,128)(4,1)} fusion(s32[8]{0:T(128)} %bitcast.111), kind=kLoop, calls=%fused_computation.42 | loop fusion | flops 56 | bytes 88 | tf_op jit(solution)/shard_map/lt | solution.py:57
  35.1 3.0 %fusion.21 = f32[256,8,256]{2,0,1:T(8,128)} fusion(bf16[1,8,256,128]{3,2,1,0:T(8,128)(2,1)S(1)} %copy-done, bf16[3,128,256]{2,1,0:T(8,128)(2,1)S(1)} %gather_fusion.1, pred[3]{0:T(512)(128)(4,1)S(1)} %iota_compare_fusion.3, bf16[1,1,3,128,128]{4,3,2,1,0:T(8,128)(2,1)} %param.23), kind=kOutput, calls=%fused_computation.23 | convolution fusion | flops 159514624 | bytes 2916355 | tf_op jit(solution)/shard_map/liq,qn->lin/dot_general | solution.py:74
  38.1 1.2 %broadcast_select_fusion = f32[128]{0:T(128)} fusion(pred[128]{0:T(512)(128)(4,1)} %lt.160, f32[128]{0:T(128)} %squeeze.47), kind=kLoop, calls=%fused_computation.55 | loop fusion | flops 128 | bytes 1152 | tf_op jit(solution)/shard_map/jit(_where)/select_n | solution.py:102
  39.4 0.9 constant_dynamic-update-slice_fusion.1
  40.2 0.9 constant_dynamic-update-slice_fusion
  41.1 0.9 constant_dynamic-update-slice_fusion.2
  42.1 6.6 %collective-permute-start.5 = (bf16[4,16,4,256]{3,2,1,0:T(4,128)(2,1)S(1)}, bf16[4,16,4,256]{3,2,1,0:T(4,128)(2,1)S(1)}, u32[]{:S(2)}, u32[]{:S(2)}) collective-permute-start(bf16[4,16,4,256]{3,2,1,0:T(4,128)(2,1)S(1)} %get-tuple-element.7), channel_id=1, source_target_pairs={{0,4},{4,8},{8,12},{12,16},{16,20},{20,24},{24,28},{1,5},{5,9},{9,... | collective-permute-start | bytes 393224 | tf_op jit(solution)/shard_map/ppermute | solution.py:25
  48.8 1.9 %collective-permute-start.6 = (bf16[4,16,4,256]{3,2,1,0:T(4,128)(2,1)S(1)}, bf16[4,16,4,256]{3,2,1,0:T(4,128)(2,1)S(1)}, u32[]{:S(2)}, u32[]{:S(2)}) collective-permute-start(bf16[4,16,4,256]{3,2,1,0:T(4,128)(2,1)S(1)} %get-tuple-element.8), channel_id=1, source_target_pairs={{4,0},{8,4},{12,8},{16,12},{20,16},{24,20},{28,24},{5,1},{9,5},{13... | collective-permute-start | bytes 393224 | tf_op jit(solution)/shard_map/ppermute | solution.py:25
  50.9 4.2 %collective-permute-done.6 = bf16[4,16,4,256]{3,2,1,0:T(4,128)(2,1)S(1)} collective-permute-done((bf16[4,16,4,256]{3,2,1,0:T(4,128)(2,1)S(1)}, bf16[4,16,4,256]{3,2,1,0:T(4,128)(2,1)S(1)}, u32[]{:S(2)}, u32[]{:S(2)}) %collective-permute-start.6) | collective-permute-done | bytes 131104 | tf_op jit(solution)/shard_map/ppermute | solution.py:25
  55.2 0.8 fusion.22
  56.0 1.6 %broadcast_in_dim.83 = f32[512,4,256]{2,1,0:T(4,128)} broadcast(f32[]{:T(128)} %constant.19.clone.1), dimensions={} | broadcast | bytes 2097156 | tf_op jit(solution)/shard_map/broadcast_in_dim | solution.py:107
  57.7 13.6 %scatter_fusion = f32[512,4,256]{2,1,0:T(4,128)} fusion(f32[512,4,256]{2,1,0:T(4,128)} %broadcast_in_dim.83, s32[128]{0:T(128)S(1)} %fusion.34, f32[128,4,256]{2,1,0:T(4,128)S(1)} %fusion.22), kind=kCustom, calls=%fused_computation.3 | custom fusion | flops 131072 | bytes 1573376 | tf_op jit(solution)/shard_map/scatter-add | solution.py:109
  71.2 2.0 %copy.36 = f32[512,4,256]{2,0,1:T(8,128)S(1)} copy(f32[512,4,256]{2,1,0:T(4,128)} %scatter_fusion) | data formatting | bytes 4194304 | tf_op jit(solution)/shard_map/scatter-add | solution.py:109
  73.2 1.5 %copy.37 = f32[8,4,64,256]{3,2,1,0:T(8,128)} copy(f32[8,4,64,256]{3,2,0,1:T(8,128)S(1)} %bitcast.100) | data formatting | bytes 4194304 | tf_op jit(solution)/shard_map/transpose | solution.py:113
  74.7 2.9 %copy.38 = f32[8,256,256]{1,2,0:T(8,128)} copy(f32[8,256,256]{2,1,0:T(8,128)} %bitcast.101) | data formatting | bytes 4194304 | tf_op jit(solution)/shard_map/reshape | solution.py:114
  77.6 0.7 copy-done.2
  78.4 1.3 %pad_maximum_fusion = bf16[14,256,256]{1,2,0:T(8,128)(2,1)S(1)} fusion(bf16[3,256,256]{1,2,0:T(8,128)(2,1)} %collective-permute-done.1, bf16[8,256,256]{1,2,0:T(8,128)(2,1)S(1)} %bitcast_select_fusion, bf16[3,256,256]{1,2,0:T(8,128)(2,1)} %copy-done.2), kind=kLoop, calls=%fused_computation.13 | loop fusion | flops 1835008 | bytes 3670016 | tf_op jit(solution)/shard_map/concatenate | solution.py:18
  79.7 5.2 %gather_fusion = bf16[56,256,256]{1,2,0:T(8,128)(2,1)} fusion(bf16[14,256,256]{1,2,0:T(8,128)(2,1)S(1)} %pad_maximum_fusion, s32[1024]{0:T(1024)S(1)} %pad_clamp_fusion.2), kind=kCustom, calls=%fused_computation | custom fusion | bytes 14680288 | tf_op jit(solution)/shard_map/gather | solution.py:55
  84.9 8.6 %fusion.12 = bf16[1,8,256,256]{2,3,1,0:T(8,128)(2,1)S(1)} fusion(f32[8,256,256]{1,2,0:T(8,128)} %copy.38, f32[256,8,256]{2,0,1:T(8,128)} %fusion.21, bf16[1,8,7,256,256]{4,3,2,1,0:T(8,128)(2,1)} %param.19, bf16[8,7,256,256]{2,3,1,0:T(8,128)(2,1)} %bitcast.102, pred[8,7]{1,0:T(8,128)(4,1)S(1)} %copy-done.9, pred[8,256]{1,0:T(8,128)(4,1)S(1)} %tile.9), kind=kOutput, calls=%fused_computation.14 | convolution fusion | flops 1884815360 | bytes 19925048 | tf_op jit(solution)/shard_map/lsij,lsjn->lin/dot_general | solution.py:59
  93.5 1.3 %copy.39 = bf16[1,8,256,256]{3,2,1,0:T(8,128)(2,1)} copy(bf16[1,8,256,256]{2,3,1,0:T(8,128)(2,1)S(1)} %fusion.12) | data formatting | bytes 2097152 | tf_op jit(solution)/shard_map/broadcast_in_dim | solution.py:120
  (51 shorter events, 3.6 us)
Async XLA Ops:
  0.0 35.1 %copy-start = (bf16[1,8,256,128]{3,2,1,0:T(8,128)(2,1)S(1)}, bf16[1,8,256,128]{3,2,1,0:T(8,128)(2,1)}, u32[]{:S(2)}) copy-start(bf16[1,8,256,128]{3,2,1,0:T(8,128)(2,1)} %param.24) | copy-start | bytes 1572868
  2.2 0.9 copy-start.5
  2.3 5.9 %copy-start.1 = (bf16[1,8,256,256]{3,2,1,0:T(8,128)(2,1)S(1)}, bf16[1,8,256,256]{3,2,1,0:T(8,128)(2,1)}, u32[]{:S(2)}) copy-start(bf16[1,8,256,256]{3,2,1,0:T(8,128)(2,1)} %param.15) | copy-start | bytes 3145732
  4.9 34.5 %collective-permute-start.2 = (bf16[2,1,16,4,256]{4,3,2,1,0:T(4,128)(2,1)}, bf16[2,1,16,4,256]{4,3,2,1,0:T(4,128)(2,1)}, u32[]{:S(2)}, u32[]{:S(2)}) collective-permute-start(bf16[2,1,16,4,256]{4,3,2,1,0:T(4,128)(2,1)} %get-tuple-element.11), channel_id=1, source_target_pairs={{0,1},{1,0},{2,3},{3,2},{4,5},{5,4},{6,7},{7,6},{8,9},{9,8},{10,11... | collective-permute-start | bytes 196616 | tf_op jit(solution)/shard_map/ppermute | solution.py:92
  6.9 33.3 %collective-permute-start.3 = (bf16[2,1,16,4,256]{4,3,2,1,0:T(4,128)(2,1)}, bf16[2,1,16,4,256]{4,3,2,1,0:T(4,128)(2,1)}, u32[]{:S(2)}, u32[]{:S(2)}) collective-permute-start(bf16[2,1,16,4,256]{4,3,2,1,0:T(4,128)(2,1)} %get-tuple-element.10), channel_id=1, source_target_pairs={{0,2},{1,3},{2,0},{3,1},{4,6},{5,7},{6,4},{7,5},{8,10},{9,11},{10,... | collective-permute-start | bytes 196616 | tf_op jit(solution)/shard_map/ppermute | solution.py:92
  8.2 33.0 %collective-permute-start.4 = (bf16[2,1,16,4,256]{4,3,2,1,0:T(4,128)(2,1)}, bf16[2,1,16,4,256]{4,3,2,1,0:T(4,128)(2,1)}, u32[]{:S(2)}, u32[]{:S(2)}) collective-permute-start(bf16[2,1,16,4,256]{4,3,2,1,0:T(4,128)(2,1)} %get-tuple-element.9), channel_id=1, source_target_pairs={{0,3},{1,2},{2,1},{3,0},{4,7},{5,6},{6,5},{7,4},{8,11},{9,10},{10,... | collective-permute-start | bytes 196616 | tf_op jit(solution)/shard_map/ppermute | solution.py:92
  8.7 4.9 %copy-start.7 = (s32[1,1,2,4]{3,2,1,0:T(2,128)S(1)}, s32[1,1,2,4]{3,2,1,0:T(2,128)}, u32[]{:S(2)}) copy-start(s32[1,1,2,4]{3,2,1,0:T(2,128)} %param.27) | copy-start | bytes 100
  8.7 5.7 %copy-start.3 = (f32[1,1,2,4,16]{4,3,2,1,0:T(4,128)S(1)}, f32[1,1,2,4,16]{4,3,2,1,0:T(4,128)}, u32[]{:S(2)}) copy-start(f32[1,1,2,4,16]{4,3,2,1,0:T(4,128)} %param.28) | copy-start | bytes 1540
  8.9 25.6 %copy-start.6 = (s32[1,8,7]{1,0,2:T(1,128)S(1)}, s32[1,8,7]{1,0,2:T(1,128)}, u32[]{:S(2)}) copy-start(s32[1,8,7]{1,0,2:T(1,128)} %param.17) | copy-start | bytes 676
  9.0 68.6 %collective-permute-start = (bf16[3,256,256]{1,2,0:T(8,128)(2,1)S(1)}, bf16[3,256,256]{1,2,0:T(8,128)(2,1)S(1)}, u32[]{:S(2)}, u32[]{:S(2)}) collective-permute-start(bf16[3,256,256]{1,2,0:T(8,128)(2,1)S(1)} %get-tuple-element.5), channel_id=1, source_target_pairs={{0,1},{1,2},{2,3},{4,5},{5,6},{6,7},{8,9},{9,10},{10,11},{12,13},{... | collective-permute-start | bytes 1179656 | tf_op jit(solution)/shard_map/ppermute | solution.py:14
  12.3 66.0 %collective-permute-start.1 = (bf16[3,256,256]{1,2,0:T(8,128)(2,1)S(1)}, bf16[3,256,256]{1,2,0:T(8,128)(2,1)}, u32[]{:S(2)}, u32[]{:S(2)}) collective-permute-start(bf16[3,256,256]{1,2,0:T(8,128)(2,1)S(1)} %get-tuple-element.6), channel_id=1, source_target_pairs={{1,0},{2,1},{3,2},{5,4},{6,5},{7,6},{9,8},{10,9},{11,10},{13,12},{... | collective-permute-start | bytes 1179656 | tf_op jit(solution)/shard_map/ppermute | solution.py:17
  16.4 22.8 %copy-start.4 = (s32[1,1,2,4,16]{4,3,2,1,0:T(4,128)S(1)}, s32[1,1,2,4,16]{4,3,2,1,0:T(4,128)}, u32[]{:S(2)}) copy-start(s32[1,1,2,4,16]{4,3,2,1,0:T(4,128)} %param.26) | copy-start | bytes 1540
  35.1 20.1 %copy-start.8 = (f32[4]{0:T(128)S(1)}, f32[4]{0:T(128)}, u32[]{:S(2)}) copy-start(f32[4]{0:T(128)} %constant.4.clone) | copy-start | bytes 52
  42.1 8.7 %collective-permute-start.5 = (bf16[4,16,4,256]{3,2,1,0:T(4,128)(2,1)S(1)}, bf16[4,16,4,256]{3,2,1,0:T(4,128)(2,1)S(1)}, u32[]{:S(2)}, u32[]{:S(2)}) collective-permute-start(bf16[4,16,4,256]{3,2,1,0:T(4,128)(2,1)S(1)} %get-tuple-element.7), channel_id=1, source_target_pairs={{0,4},{4,8},{8,12},{12,16},{16,20},{20,24},{24,28},{1,5},{5,9},{9,... | collective-permute-start | bytes 393224 | tf_op jit(solution)/shard_map/ppermute | solution.py:25
  48.8 6.3 %collective-permute-start.6 = (bf16[4,16,4,256]{3,2,1,0:T(4,128)(2,1)S(1)}, bf16[4,16,4,256]{3,2,1,0:T(4,128)(2,1)S(1)}, u32[]{:S(2)}, u32[]{:S(2)}) collective-permute-start(bf16[4,16,4,256]{3,2,1,0:T(4,128)(2,1)S(1)} %get-tuple-element.8), channel_id=1, source_target_pairs={{4,0},{8,4},{12,8},{16,12},{20,16},{24,20},{28,24},{5,1},{9,5},{13... | collective-permute-start | bytes 393224 | tf_op jit(solution)/shard_map/ppermute | solution.py:25
  77.6 0.7 copy-start.2
  79.7 5.3 %copy-start.9 = (pred[8,7]{1,0:T(8,128)(4,1)S(1)}, pred[8,7]{1,0:T(8,128)(4,1)}, u32[]{:S(2)}) copy-start(pred[8,7]{1,0:T(8,128)(4,1)} %iota_compare_fusion.1) | copy-start | bytes 172
